TPU v7x, 32 devices: a whole 2x2x4 slice. The times are simulated.
32 devices in a mesh: ctx: 8 (over y, x, core), chan: 4 (over z).
Axes of the slice: x: 2, y: 2, z: 4, core: 2. Of those that a mesh axis runs over, the one named last changes fastest.
Arguments:
- features: bfloat16 [3, 8192, 4096], P(None, 'chan', 'ctx'), may hold values from -6 to 6
- short_filter: float32 [3, 3, 8192], P(None, None, 'chan'), may hold values from -3.5 to 3.5
- lengths: int32 [8], P('ctx'), may hold values from 64 to 512, as said below
- offsets: int32 [8], P('ctx'), may hold values from 0 to 8128, as said below
- decay_rates: float32 [16, 1024], P(None, 'chan'), may hold values from 0 to 1, as said below
- residues: float32 [16, 1024], P(None, 'chan'), may hold values from -1 to 1
- skip_weight: float32 [8192], P('chan'), may hold values from -1 to 1
- out_weight: bfloat16 [8192, 4096], P('chan'), may hold values from -0.09375 to 0.09375
Outputs:
- projected: bfloat16 [4096, 4096], P('chan', 'ctx')
Inputs may be any that keep to these rules, and one draw needn't show every extreme that they name: `lengths`: used slots of each shard, counted from slot 0; some shard uses all 512 slots and some only 64. offsets[i] + lengths[i] <= offsets[i + 1]; the first offset is 0. `decay_rates`: positive rates.
All inputs are finite; a program needn't handle non-finite values.
Results may differ from a plain program's by a relative error of at most 0.018.
Values may be sent and summed in bfloat16 or wider, within the bound.
No kernel may reach another device: no remote copies, remote signals or barrier semaphores. Data moves between devices by JAX's collectives and lax.ppermute only.
A program may use at most 192 MiB of HBM per device.

v0:
```python
import jax
import jax.numpy as jnp
from jax import lax
from jax.sharding import PartitionSpec as P

highest = lax.Precision.HIGHEST


def passed_along(array, axis, by):
    length = lax.axis_size(axis)
    pairs = [(i, i + by) for i in range(length) if 0 <= i + by < length]
    return lax.ppermute(array, axis, pairs)


def shortened(array):
    return jax.tree.map(lambda a: a.astype(jnp.bfloat16) if a.dtype == jnp.float32 else a, array)


def block_pass(blocks, firsts, counts, decay_rows, residue):
    groups, per_group, block_count, block_width = blocks.shape
    mode_count = decay_rows.shape[0]
    rate_g = decay_rows.T
    residue_g = residue.T
    lag_index = jnp.arange(block_width)
    lag_float = lag_index.astype(jnp.float32)
    to_end = jnp.exp(-rate_g[:, None, :] * (block_width - 1.0 - lag_float)[None, :, None])
    raw_sums = lax.dot_general(
        blocks.reshape(groups, per_group * block_count, block_width),
        to_end,
        (((2,), (1,)), ((0,), (0,))),
        precision=highest,
    )
    lift = jnp.exp(rate_g[:, None, :] * (block_width - counts.astype(jnp.float32))[None, :, None])
    summary = raw_sums.reshape(groups, per_group, block_count, mode_count) * lift[:, None, :, :]
    difference = (lag_index[:, None] - lag_index[None, :]).astype(jnp.float32)
    distance = jnp.maximum(difference, 0.0)
    toeplitz = jnp.zeros((groups, block_width, block_width), jnp.float32)
    for mode_index in range(mode_count):
        toeplitz = toeplitz + residue_g[:, mode_index, None, None] * jnp.exp(
            -rate_g[:, mode_index, None, None] * distance[None]
        )
    toeplitz = jnp.where((difference >= 0.0)[None], toeplitz, 0.0)
    inner_part = lax.dot_general(blocks, toeplitz, (((3,), (2,)), ((0,), (0,))), precision=highest)
    lasts = firsts + counts.astype(jnp.float32) - 1.0
    gap_matrix = jnp.maximum(firsts[None, :] - lasts[:, None], 0.0)
    earlier_mask = lag_index[:block_count, None] < lag_index[None, :block_count]
    mixing = jnp.where(
        earlier_mask[None, None], jnp.exp(-rate_g[:, :, None, None] * gap_matrix[None, None]), 0.0
    )
    entering = jnp.einsum("gkcm,gmcb->gkbm", summary, mixing, precision=highest)
    return (inner_part, summary, entering, lasts)


def outer_pass(entering, decay_rows, residue, block_width):
    groups, per_group, block_count, mode_count = entering.shape
    rate_g = decay_rows.T
    lag_float = jnp.arange(block_width, dtype=jnp.float32)
    spread_values = residue.T[:, :, None] * jnp.exp(-rate_g[:, :, None] * lag_float[None, None, :])
    outer_part = lax.dot_general(
        entering.reshape(groups, per_group * block_count, mode_count),
        spread_values,
        (((2,), (1,)), ((0,), (0,))),
        precision=highest,
    )
    return outer_part.reshape(groups, per_group, block_count, block_width)


def shards(
    features, short_filter, lengths, offsets, decay_rates, residues, skip_weight, out_weight
):
    kernel_taps = short_filter.shape[1]
    channels = features.shape[1]
    slot_count = features.shape[2]
    groups = decay_rates.shape[1]
    per_group = channels // groups
    block_width = min(128, slot_count)
    length = lengths[0]
    tail_rows = lax.dynamic_slice_in_dim(
        features, length - (kernel_taps - 1), kernel_taps - 1, axis=2
    )
    previous = passed_along(tail_rows, "ctx", 1)
    extended = jnp.concatenate([previous, features], axis=2)
    short_conv = jnp.zeros((3, channels, slot_count), jnp.float32)
    for tap_index in range(kernel_taps):
        window_rows = lax.slice_in_dim(
            extended, kernel_taps - 1 - tap_index, kernel_taps - 1 - tap_index + slot_count, axis=2
        )
        short_conv = short_conv + short_filter[:, tap_index, :, None] * window_rows.astype(
            jnp.float32
        )
    usable = jnp.arange(slot_count) < length
    product = jnp.where(usable, short_conv[1] * short_conv[2], 0.0)
    all_lengths, all_offsets = (
        lax.all_gather(lengths, "ctx", axis=0, tiled=True),
        lax.all_gather(offsets, "ctx", axis=0, tiled=True),
    )
    ctx_count = lax.axis_size("ctx")
    rank_self = lax.axis_index("ctx")
    shared = groups // ctx_count
    decay_mine = lax.dynamic_slice_in_dim(decay_rates, rank_self * shared, shared, 1)
    residue_mine = lax.dynamic_slice_in_dim(residues, rank_self * shared, shared, 1)
    per_shard = slot_count // block_width
    within = jnp.tile(jnp.arange(per_shard) * block_width, ctx_count)
    firsts_all = jnp.repeat(all_offsets, per_shard).astype(jnp.float32) + within.astype(jnp.float32)
    counts_all = jnp.clip(jnp.repeat(all_lengths, per_shard) - within, 0, block_width)
    received = lax.all_to_all(
        product.reshape(groups, per_group, slot_count).astype(jnp.bfloat16),
        "ctx",
        split_axis=0,
        concat_axis=2,
        tiled=True,
    ).astype(jnp.float32)
    item_count = received.shape[1]
    blocks = received.reshape(shared, item_count, ctx_count * per_shard, block_width)
    inner_part, summary, entering, lasts = block_pass(
        blocks, firsts_all, counts_all, decay_mine, residue_mine
    )
    outer_part = outer_pass(entering, decay_mine, residue_mine, block_width)
    result = (inner_part + outer_part).reshape(shared, item_count, ctx_count * slot_count)
    long_conv = lax.all_to_all(
        shortened(result), "ctx", split_axis=2, concat_axis=0, tiled=True
    ).astype(result.dtype)
    long_conv = long_conv.reshape(channels, slot_count)
    mixed_rows = jnp.where(
        usable, short_conv[0] * (long_conv + skip_weight[:, None] * product), 0.0
    ).astype(jnp.bfloat16)
    return lax.psum_scatter(
        lax.dot_general(
            out_weight, mixed_rows, (((0,), (0,)), ((), ())), preferred_element_type=jnp.float32
        ).astype(jnp.bfloat16),
        "chan",
        scatter_dimension=0,
        tiled=True,
    )


def solution(mesh):
    placed = (
        P(None, "chan", "ctx"),
        P(None, None, "chan"),
        P("ctx"),
        P("ctx"),
        P(None, "chan"),
        P(None, "chan"),
        P("chan"),
        P("chan", None),
    )
    return jax.shard_map(
        shards, mesh=mesh, in_specs=placed, out_specs=P("chan", "ctx"), check_vma=False
    )
```

profile of v0, /device:TPU:0, one launch (start us, length us, event | category | flops | bytes accessed | tf_op | source)
XLA Modules:
  0.0 309.9 jit_solution(4460304330251844339)
XLA Ops:
  7.2 2.5 constant_dynamic-slice_fusion
  10.6 2.4 collective-permute-start
  15.8 9.1 %all-reduce.2 = (s32[8]{0:T(128)S(1)}, s32[8]{0:T(128)S(1)}) all-reduce(s32[8]{0:T(128)S(1)} %dynamic-update-slice, s32[8]{0:T(128)S(1)} %dynamic-update-slice.1), channel_id=1, replica_groups=mesh['ctx'=8,'chan'=4] {'ctx'}, use_global_device_ids=true, to_apply=%add | all-reduce | flops 16 | bytes 128
  26.0 12.5 %multiply_add_fusion = f32[3,2048,512]{2,1,0:T(8,128)S(1)} fusion(bf16[3,2048,512]{2,1,0:T(8,128)(2,1)} %param.8, bf16[3,2048,2]{2,1,0:T(8,128)(2,1)S(1)} %copy.38, f32[3,2048]{1,0:T(4,128)S(1)} %get-tuple-element.46, f32[3,2048]{1,0:T(4,128)S(1)} %get-tuple-element.47, f32[3,2048]{1,0:T(4,128)S(1)} %bitcast.143), kind=kLoop, calls=%fused_computation.1 | loop fusion | flops 44040192 | bytes 18972672 | tf_op jit(solution)/shard_map/add | solution.py:88
  38.5 4.5 %copy-done.2 = f32[3,2048,512]{2,1,0:T(8,128)} copy-done((f32[3,2048,512]{2,1,0:T(8,128)}, f32[3,2048,512]{2,1,0:T(8,128)S(1)}, u32[]{:S(2)}) %copy-start.2) | copy-done | bytes 12582936
  43.1 2.5 fusion.11
  45.5 3.7 %all-to-all-start = ((bf16[256,8,512]{2,1,0:T(8,128)(2,1)}), bf16[256,8,512]{2,1,0:T(8,128)(2,1)S(1)}, u32[]{:S(2)}, u32[]{:S(2)}) async-start(bf16[256,8,512]{2,1,0:T(8,128)(2,1)} %fusion.11), calls=%async_computation | async-start | bytes 4194304 | tf_op jit(solution)/shard_map/all_to_all | solution.py:106
  50.3 25.6 %all-to-all-done = bf16[256,8,512]{2,1,0:T(8,128)(2,1)S(1)} async-done(((bf16[256,8,512]{2,1,0:T(8,128)(2,1)}), bf16[256,8,512]{2,1,0:T(8,128)(2,1)S(1)}, u32[]{:S(2)}, u32[]{:S(2)}) %all-to-all-start) | async-done | bytes 2097184 | tf_op jit(solution)/shard_map/all_to_all | solution.py:106
  77.2 3.3 %copy.39 = bf16[32,8,8,512]{3,2,1,0:T(8,128)(2,1)S(1)} copy(bf16[32,8,8,512]{3,1,0,2:T(8,128)(2,1)} %bitcast.141) | data formatting | bytes 4194304 | tf_op jit(solution)/shard_map/all_to_all | solution.py:106
  80.5 2.8 reshape_reshape.3
  83.3 2.6 reshape.334
  85.9 3.4 %fusion.128 = f32[32,256,16]{1,2,0:T(8,128)S(1)} fusion(bf16[32,256,128]{2,1,0:T(8,128)(2,1)} %reshape_reshape.3, f32[128]{0:T(128)S(1)} %convert_subtract_fusion, f32[32,16]{1,0:T(8,128)S(1)} %copy.40), kind=kOutput, calls=%fused_computation.136 | convolution fusion | flops 201392128 | bytes 2624000 | tf_op jit(solution)/shard_map/dot_general | solution.py:27
  89.7 17.6 %fusion.82 = f32[32,8,32,16]{2,1,3,0:T(8,128)} fusion(f32[32,8,32,16]{2,1,3,0:T(8,128)S(1)} %reshape.335, f32[32,32]{1,0:T(8,128)S(1)} %subtract_maximum_fusion, f32[32,16]{1,0:T(8,128)S(1)} %copy.40, pred[32,32]{1,0:T(8,128)(4,1)S(1)} %broadcast_compare_fusion, f32[32,32,16]{1,2,0:T(8,128)S(1)} %multiply_exponential_fusion), kind=kOutput, calls=%fused_computation.93 | convolution fusion | flops 51511296 | bytes 1121280 | tf_op jit(solution)/shard_map/gkcm,gmcb->gkbm/dot_general | solution.py:50
  109.5 7.5 %fusion.123 = f32[32,256,128]{2,1,0:T(8,128)S(1)} fusion(f32[32,256,16]{1,2,0:T(8,128)S(1)} %reshape.336, f32[32,16]{1,0:T(8,128)S(1)} %copy.40, f32[32,16]{1,0:T(8,128)S(1)} %copy.44), kind=kOutput, calls=%fused_computation.130 | convolution fusion | flops 201457664 | bytes 4722688 | tf_op jit(solution)/shard_map/dot_general | solution.py:59
  117.0 9.5 %add_convert_fusion = bf16[32,8,32,128]{3,2,1,0:T(8,128)(2,1)S(1)} fusion(f32[32,8,32,128]{3,2,1,0:T(8,128)S(1)} %bitcast.142, bf16[32,8,32,128]{3,2,1,0:T(8,128)(2,1)S(1)} %copy-done.4, f32[32]{0:T(128)S(1)} %get-tuple-element.29, f32[32]{0:T(128)S(1)} %get-tuple-element.13, f32[32]{0:T(128)S(1)} %get-tuple-element.30, f32[32]{0:T(128)S(1)} %get-tuple-element.14, ...), kind=kOutput, calls=%fused_computation.22 | convolution fusion | flops 1637875712 | bytes 8474624 | tf_op jit(solution)/shard_map/dot_general | solution.py:43
  126.5 6.8 %copy.50 = bf16[32,8,32,128]{0,1,3,2:T(8,128)(2,1)} copy(bf16[32,8,32,128]{3,2,1,0:T(8,128)(2,1)S(1)} %add_convert_fusion) | data formatting | bytes 4194304 | tf_op jit(solution)/shard_map/convert_element_type | solution.py:16
  133.3 10.1 %reshape.351 = bf16[8,2,65536]{2,1,0:T(2,128)(2,1)S(1)} reshape(bf16[4096,8,32]{2,1,0:T(8,128)(2,1)} %bitcast.140) | data formatting | bytes 4194304
  143.5 29.8 %all_to_all.24 = bf16[8,2,65536]{2,1,0:T(2,128)(2,1)} all-to-all(bf16[8,2,65536]{2,1,0:T(2,128)(2,1)S(1)} %reshape.351), channel_id=1, replica_groups=mesh['ctx'=8,'chan'=4] {'ctx'}, dimensions={0} | all-to-all | bytes 4194304 | tf_op jit(solution)/shard_map/all_to_all | solution.py:120
  173.2 8.7 %reshape.352 = bf16[4096,8,32]{2,1,0:T(8,128)(2,1)} reshape(bf16[8,2,65536]{2,1,0:T(2,128)(2,1)} %all_to_all.24) | data formatting | bytes 4194304
  181.9 10.2 %convert_bitcast_fusion = f32[8,32,8,512]{1,2,3,0:T(8,128)} fusion(bf16[32,8,8,512]{0,1,3,2:T(8,128)(2,1)} %bitcast.139), kind=kLoop, calls=%fused_computation | loop fusion | flops 1048576 | bytes 6291456 | tf_op jit(solution)/shard_map/convert_element_type | solution.py:122
  192.1 12.0 %copy.47 = f32[8,32,8,512]{3,2,1,0:T(8,128)} copy(f32[8,32,8,512]{1,2,3,0:T(8,128)} %convert_bitcast_fusion) | data formatting | bytes 8388608 | tf_op jit(solution)/shard_map/convert_element_type | solution.py:122
  204.1 6.4 %fusion.8 = bf16[2048,512]{1,0:T(8,128)(2,1)S(1)} fusion(f32[3,2048,512]{2,1,0:T(8,128)} %copy-done.2, f32[8,32,8,512]{3,2,1,0:T(8,128)} %copy.47, f32[2048]{0:T(1024)S(1)} %copy-done.6, pred[512]{0:T(512)(128)(4,1)S(1)} %iota_compare_fusion), kind=kLoop, calls=%fused_computation.16 | loop fusion | flops 7340032 | bytes 18883072 | tf_op jit(solution)/shard_map/convert_element_type | solution.py:126
  210.5 14.0 %fusion.5 = bf16[4096,512]{0,1:T(8,128)(2,1)} fusion(bf16[2048,512]{1,0:T(8,128)(2,1)S(1)} %fusion.8, bf16[2048,4096]{1,0:T(8,128)(2,1)} %param.15), kind=kOutput, calls=%fused_computation.11 | convolution fusion | flops 8592031744 | bytes 23068672 | tf_op jit(solution)/shard_map/dot_general | solution.py:128
  224.5 76.3 %reduce-scatter.2.cloned.1.call-done = bf16[1024,512]{0,1:T(8,128)(2,1)} async-done(((bf16[4096,512]{0,1:T(8,128)(2,1)}), bf16[1024,512]{0,1:T(8,128)(2,1)}) %reduce-scatter.2.cloned.1.call-update) | async-done | bytes 1048592 | tf_op jit(solution)/shard_map/reduce_scatter | solution.py:127
  (56 shorter events, 11.3 us)
Async XLA Ops:
  6.5 42.8 %copy-start = (f32[16,256]{1,0:T(8,128)S(1)}, f32[16,256]{1,0:T(8,128)}, u32[]{:S(2)}) copy-start(f32[16,256]{1,0:T(8,128)} %param.13) | copy-start | bytes 49156
  7.2 6.4 %copy-start.8 = (u32[32]{0:T(128)S(1)}, u32[32]{0:T(128)}, u32[]{:S(2)}) copy-start(u32[32]{0:T(128)} %constant.36) | copy-start | bytes 388
  7.2 17.6 %copy-start.5 = (f32[3,3,2048]{2,1,0:T(4,128)S(1)}, f32[3,3,2048]{2,1,0:T(4,128)}, u32[]{:S(2)}) copy-start(f32[3,3,2048]{2,1,0:T(4,128)} %param.9) | copy-start | bytes 221188
  10.6 14.5 %collective-permute-start = (bf16[3,2048,2]{1,0,2:T(4,128)(2,1)S(1)}, bf16[3,2048,2]{1,0,2:T(4,128)(2,1)S(1)}, u32[]{:S(2)}, u32[]{:S(2)}) collective-permute-start(bf16[3,2048,2]{1,0,2:T(4,128)(2,1)S(1)} %copy.54), channel_id=1, source_target_pairs={{0,4},{4,8},{8,12},{12,16},{16,20},{20,24},{24,28},{1,5},{5,9},{9,... | collective-permute-start | bytes 73736 | tf_op jit(solution)/shard_map/ppermute | solution.py:12
  38.5 4.5 %copy-start.2 = (f32[3,2048,512]{2,1,0:T(8,128)}, f32[3,2048,512]{2,1,0:T(8,128)S(1)}, u32[]{:S(2)}) copy-start(f32[3,2048,512]{2,1,0:T(8,128)S(1)} %multiply_add_fusion) | copy-start | bytes 37748740
  45.5 4.1 %copy-start.7 = (f32[16,256]{1,0:T(8,128)S(1)}, f32[16,256]{1,0:T(8,128)}, u32[]{:S(2)}) copy-start(f32[16,256]{1,0:T(8,128)} %param.12) | copy-start | bytes 49156
  45.5 30.3 %all-to-all-start = ((bf16[256,8,512]{2,1,0:T(8,128)(2,1)}), bf16[256,8,512]{2,1,0:T(8,128)(2,1)S(1)}, u32[]{:S(2)}, u32[]{:S(2)}) async-start(bf16[256,8,512]{2,1,0:T(8,128)(2,1)} %fusion.11), calls=%async_computation | async-start | bytes 4194304 | tf_op jit(solution)/shard_map/all_to_all | solution.py:106
  49.3 251.5 %reduce-scatter.2.cloned.1.call-start = ((), (), s32[]{:S(2)}) async-start(), calls=%async_computation.3 | async-start | bytes 5242880 | tf_op jit(solution)/shard_map/reduce_scatter | solution.py:127
  75.9 1.3 copy-start.3
  109.5 7.5 %copy-start.4 = (bf16[32,8,32,128]{3,2,1,0:T(8,128)(2,1)S(1)}, bf16[32,8,32,128]{3,2,1,0:T(8,128)(2,1)}, u32[]{:S(2)}) copy-start(bf16[32,8,32,128]{3,2,1,0:T(8,128)(2,1)} %reshape.334) | copy-start | bytes 6291460
  192.1 12.0 %copy-start.6 = (f32[2048]{0:T(1024)S(1)}, f32[2048]{0:T(1024)}, u32[]{:S(2)}) copy-start(f32[2048]{0:T(1024)} %param.14) | copy-start | bytes 24580
  224.5 78.6 %copy-start.1 = (f32[16,256]{1,0:T(8,128)S(1)}, f32[16,256]{1,0:T(8,128)}, u32[]{:S(2)}) copy-start(f32[16,256]{1,0:T(8,128)} %param.13) | copy-start | bytes 49156
Sparse Core Ops, SparseCore 0:
  224.6 76.1 reduce-scatter.1
where the time goes:
time: 311 us; the launch traced here: 310 us
  waiting for transfers between devices  102 us (33%)
  local copies, waits for them, and re-layouts  63.9 us (21%)
  matrix products  52 us (17%)
  blocking collectives  38.8 us (12%)
  other arithmetic  32.2 us (10%)
  between operations  15 us (5%)
  starting transfers between devices  6.13 us (2%)
    reduce_scatter x1, waiting for transfers between devices, shards(): lax.psum_scatter(lax.dot_general(out_weight, mixed_rows, (((0,), (0,)), (...  76.3 us
    all_to_all x1, blocking collectives, shards(): lax.all_to_all(shortened(result), 'ctx', split_axis=2, concat_axis=0, til...  29.8 us
    unnamed x28, local copies, waits for them, and re-layouts  27.7 us
    all_to_all x1, waiting for transfers between devices, shards(): lax.all_to_all(product.reshape(groups, per_group, slot_count).astype(jnp....  25.6 us
    dot_general x1, matrix products, block_pass(): entering = jnp.einsum('gkcm,gmcb->gkbm', summary, mixing, precision=highest)  17.6 us
    dot_general x1, matrix products, shards(): lax.dot_general(out_weight, mixed_rows, (((0,), (0,)), ((), ())), preferr...  14 us
    add x1, other arithmetic, shards(): short_conv + short_filter[:, tap_index, :, None] * window_rows.astype(jnp...  12.5 us
    convert_element_type x1, local copies, waits for them, and re-layouts, shards(): long_conv = lax.all_to_all(shortened(result), 'ctx', split_axis=2, concat...  12 us
  transfers between devices with their start and end apart: 3, of which 2 were waited for; matrix products, arithmetic and copies ran while one was open for 1% of the time, Pallas kernels for 0%

commit v1 on v0

--- a/solution.py
+++ b/solution.py
@@ -1,9 +1,44 @@
+import functools
 import jax
 import jax.numpy as jnp
 from jax import lax
 from jax.sharding import PartitionSpec as P
 
 highest = lax.Precision.HIGHEST
+
+
+def extend_screen(buf, on_dim, mine):
+    piece_out = buf.shape
+    work_now = jnp.moveaxis(
+        buf.reshape(*piece_out[:on_dim], mine, piece_out[on_dim] // mine, *piece_out[on_dim + 1 :]),
+        on_dim,
+        0,
+    )
+    return work_now
+
+
+def rest_arrays(message, ndim_at):
+    message = jnp.moveaxis(message, 0, ndim_at)
+    odd = message.shape
+    then = message.reshape(*odd[:ndim_at], odd[ndim_at] * odd[ndim_at + 1], *odd[ndim_at + 2 :])
+    return then
+
+
+def state_files(z_in, across, unit, m):
+    z_new, left_arr = (lax.axis_size(across), lax.axis_index(across))
+    long_array = extend_screen(z_in, unit, z_new)
+    slots = [long_array[left_arr]]
+    s = 1
+    while s < z_new:
+        formed = long_array[left_arr ^ s]
+        slots.append(lax.ppermute(formed, across, [(k0, k0 ^ s) for k0 in range(z_new)]))
+        s += 1
+    long_array = jnp.stack(slots, axis=0)[left_arr ^ jnp.arange(z_new)]
+    after = rest_arrays(long_array, m)
+    return after
+
+
+move_task = functools.partial(state_files, across="ctx", unit=2, m=0)
 
 
 def passed_along(array, axis, by):
@@ -117,9 +152,7 @@
     )
     outer_part = outer_pass(entering, decay_mine, residue_mine, block_width)
     result = (inner_part + outer_part).reshape(shared, item_count, ctx_count * slot_count)
-    long_conv = lax.all_to_all(
-        shortened(result), "ctx", split_axis=2, concat_axis=0, tiled=True
-    ).astype(result.dtype)
+    long_conv = move_task(shortened(result)).astype(result.dtype)
     long_conv = long_conv.reshape(channels, slot_count)
     mixed_rows = jnp.where(
         usable, short_conv[0] * (long_conv + skip_weight[:, None] * product), 0.0

time: 311 us -> 270 us (0.87)
  blocking collectives: 38.8 us -> 9.05 us
  local copies, waits for them, and re-layouts: 63.9 us -> 37.4 us
  waiting for transfers between devices: 102 us -> 124 us
  other arithmetic: 32.2 us -> 15.7 us
  matrix products: 52 us -> 57.9 us
  starting transfers between devices: 6.13 us -> 10.5 us
    all_to_all x1 -> x0, blocking collectives: 29.8 us -> none  [shards(): lax.all_to_all(shortened(result), 'ctx', split_axis=2, concat_axis=0, til...]
    ppermute x0 -> x7, waiting for transfers between devices: none -> 22.1 us  [state_files(): lax.ppermute(formed, across, [(k0, k0 ^ s) for k0 in range(z_new)])]
    unnamed x28 -> x40, local copies, waits for them, and re-layouts: 27.7 us -> 9.26 us
    convert_element_type x2 -> x0, other arithmetic: 16.6 us -> none  [the longest x1 10.2 us: shards(): long_conv = lax.all_to_all(shortened(result), 'ctx', split_axis=2, concat...]
    convert_element_type x1 -> x0, local copies, waits for them, and re-layouts: 12 us -> none  [shards(): long_conv = lax.all_to_all(shortened(result), 'ctx', split_axis=2, concat...]
    dot_general x1, matrix products: 14 us -> 19.7 us  [shards(): lax.dot_general(out_weight, mixed_rows, (((0,), (0,)), ((), ())), preferr...]
    another operation x0 -> x2, local copies, waits for them, and re-layouts: none -> 5.55 us
    ppermute x0 -> x7, starting transfers between devices: none -> 4.49 us  [state_files(): lax.ppermute(formed, across, [(k0, k0 ^ s) for k0 in range(z_new)])]
  transfers between devices with their start and end apart: 3 -> 10, of which waited for: 2 -> 5; matrix products, arithmetic and copies ran while one was open for 1% -> 1% of each run, Pallas kernels for 0% -> 0%
where the time goes in v1:
time: 270 us
  waiting for transfers between devices  124 us (46%)
  matrix products  57.9 us (21%)
  local copies, waits for them, and re-layouts  37.4 us (14%)
  other arithmetic  15.7 us (6%)
  between operations  15.1 us (6%)
  starting transfers between devices  10.5 us (4%)
  blocking collectives  9.05 us (3%)
    reduce_scatter x1, waiting for transfers between devices, shards(): lax.psum_scatter(lax.dot_general(out_weight, mixed_rows, (((0,), (0,)), (...  76.4 us
    all_to_all x1, waiting for transfers between devices, shards(): lax.all_to_all(product.reshape(groups, per_group, slot_count).astype(jnp....  25.6 us
    ppermute x7, waiting for transfers between devices, state_files(): lax.ppermute(formed, across, [(k0, k0 ^ s) for k0 in range(z_new)])  22.1 us
    dot_general x1, matrix products, shards(): lax.dot_general(out_weight, mixed_rows, (((0,), (0,)), ((), ())), preferr...  19.7 us
    dot_general x1, matrix products, block_pass(): entering = jnp.einsum('gkcm,gmcb->gkbm', summary, mixing, precision=highest)  17.7 us
    add x1, other arithmetic, shards(): short_conv + short_filter[:, tap_index, :, None] * window_rows.astype(jnp...  12.6 us
    dot_general x1, matrix products, block_pass(): lax.dot_general(blocks, toeplitz, (((3,), (2,)), ((0,), (0,))), precision...  9.67 us
    unnamed x40, local copies, waits for them, and re-layouts  9.26 us
  transfers between devices with their start and end apart: 10, of which 5 were waited for; matrix products, arithmetic and copies ran while one was open for 1% of the time, Pallas kernels for 0%

profile of v1, /device:TPU:0, one launch (start us, length us, event | category | flops | bytes accessed | tf_op | source)
XLA Modules:
  0.0 269.8 jit_solution(15902761827236050118)
XLA Ops:
  7.2 2.5 constant_dynamic-slice_fusion.8
  10.6 2.4 collective-permute-start
  15.8 9.1 %all-reduce.2 = (s32[8]{0:T(128)S(1)}, s32[8]{0:T(128)S(1)}) all-reduce(s32[8]{0:T(128)S(1)} %dynamic-update-slice, s32[8]{0:T(128)S(1)} %dynamic-update-slice.1), channel_id=1, replica_groups=mesh['ctx'=8,'chan'=4] {'ctx'}, use_global_device_ids=true, to_apply=%add | all-reduce | flops 16 | bytes 128
  26.1 12.6 %multiply_add_fusion = f32[3,2048,512]{2,1,0:T(8,128)S(1)} fusion(bf16[3,2048,512]{2,1,0:T(8,128)(2,1)} %param.8, bf16[3,2048,2]{2,1,0:T(8,128)(2,1)S(1)} %copy.32, f32[3,2048]{1,0:T(4,128)S(1)} %get-tuple-element.54, f32[3,2048]{1,0:T(4,128)S(1)} %get-tuple-element.55, f32[3,2048]{1,0:T(4,128)S(1)} %bitcast.184), kind=kLoop, calls=%fused_computation.1 | loop fusion | flops 44040192 | bytes 18972672 | tf_op jit(solution)/shard_map/add | solution.py:123
  38.7 4.5 %copy-done.2 = f32[3,2048,512]{2,1,0:T(8,128)} copy-done((f32[3,2048,512]{2,1,0:T(8,128)}, f32[3,2048,512]{2,1,0:T(8,128)S(1)}, u32[]{:S(2)}) %copy-start.2) | copy-done | bytes 12582936
  43.2 2.5 fusion.10
  45.7 3.6 %all-to-all-start = ((bf16[256,8,512]{2,1,0:T(8,128)(2,1)}), bf16[256,8,512]{2,1,0:T(8,128)(2,1)S(1)}, u32[]{:S(2)}, u32[]{:S(2)}) async-start(bf16[256,8,512]{2,1,0:T(8,128)(2,1)} %fusion.10), calls=%async_computation | async-start | bytes 4194304 | tf_op jit(solution)/shard_map/all_to_all | solution.py:141
  50.2 25.6 %all-to-all-done = bf16[256,8,512]{2,1,0:T(8,128)(2,1)S(1)} async-done(((bf16[256,8,512]{2,1,0:T(8,128)(2,1)}), bf16[256,8,512]{2,1,0:T(8,128)(2,1)S(1)}, u32[]{:S(2)}, u32[]{:S(2)}) %all-to-all-start) | async-done | bytes 2097184 | tf_op jit(solution)/shard_map/all_to_all | solution.py:141
  77.2 3.3 %copy.33 = bf16[32,8,8,512]{3,2,1,0:T(8,128)(2,1)S(1)} copy(bf16[32,8,8,512]{3,1,0,2:T(8,128)(2,1)} %bitcast.174) | data formatting | bytes 4194304 | tf_op jit(solution)/shard_map/all_to_all | solution.py:141
  80.5 2.8 %reshape_reshape.3 = bf16[32,256,128]{2,1,0:T(8,128)(2,1)} reshape(bf16[32,8,8,512]{3,2,1,0:T(8,128)(2,1)S(1)} %copy.33) | data formatting | bytes 4194304 | tf_op jit(solution)/shard_map/reshape;reshape | solution.py:63
  83.2 2.6 reshape.366
  85.9 3.4 %fusion.132 = f32[32,256,16]{1,2,0:T(8,128)S(1)} fusion(bf16[32,256,128]{2,1,0:T(8,128)(2,1)} %reshape_reshape.3, f32[128]{0:T(128)S(1)} %convert_subtract_fusion, f32[32,16]{1,0:T(8,128)S(1)} %copy.34), kind=kOutput, calls=%fused_computation.155 | convolution fusion | flops 201392128 | bytes 2624000 | tf_op jit(solution)/shard_map/dot_general | solution.py:62
  89.7 17.7 %fusion.85 = f32[32,8,32,16]{2,1,3,0:T(8,128)} fusion(f32[32,8,32,16]{2,1,3,0:T(8,128)S(1)} %reshape.367, f32[32,32]{1,0:T(8,128)S(1)} %subtract_maximum_fusion, f32[32,16]{1,0:T(8,128)S(1)} %copy.34, pred[32,32]{1,0:T(8,128)(4,1)S(1)} %broadcast_compare_fusion, f32[32,32,16]{1,2,0:T(8,128)S(1)} %multiply_exponential_fusion), kind=kOutput, calls=%fused_computation.96 | convolution fusion | flops 51511296 | bytes 1121280 | tf_op jit(solution)/shard_map/gkcm,gmcb->gkbm/dot_general | solution.py:85
  107.4 2.1 reshape.368
  109.5 7.5 %fusion.127 = f32[32,256,128]{2,1,0:T(8,128)S(1)} fusion(f32[32,256,16]{1,2,0:T(8,128)S(1)} %reshape.368, f32[32,16]{1,0:T(8,128)S(1)} %copy.34, f32[32,16]{1,0:T(8,128)S(1)} %copy.38), kind=kOutput, calls=%fused_computation.149 | convolution fusion | flops 201457664 | bytes 4722688 | tf_op jit(solution)/shard_map/dot_general | solution.py:94
  117.1 9.7 %add_convert_fusion = bf16[32,8,32,128]{3,2,1,0:T(8,128)(2,1)} fusion(f32[32,8,32,128]{3,2,1,0:T(8,128)S(1)} %bitcast.175, bf16[32,8,32,128]{3,2,1,0:T(8,128)(2,1)S(1)} %copy-done.4, f32[32]{0:T(128)S(1)} %get-tuple-element.37, f32[32]{0:T(128)S(1)} %get-tuple-element.21, f32[32]{0:T(128)S(1)} %get-tuple-element.38, f32[32]{0:T(128)S(1)} %get-tuple-element.22, ...), kind=kOutput, calls=%fused_computation.22 | convolution fusion | flops 1637875712 | bytes 8474624 | tf_op jit(solution)/shard_map/dot_general | solution.py:78
  126.7 3.1 %convert_element_type.137 = bf16[32,8,8,512]{3,2,1,0:T(8,128)(2,1)S(1)} reshape(bf16[32,8,32,128]{3,2,1,0:T(8,128)(2,1)} %add_convert_fusion) | data formatting | bytes 4194304 | tf_op jit(solution)/shard_map/convert_element_type | solution.py:51
  129.8 5.5 %constant_dynamic-slice_fusion = (bf16[32,8,1,512]{3,2,1,0:T(2,128)(2,1)S(1)}, bf16[32,8,1,512]{3,2,1,0:T(2,128)(2,1)S(1)}, bf16[32,8,1,512]{3,2,1,0:T(2,128)(2,...) fusion(bf16[32,8,8,512]{3,2,1,0:T(8,128)(2,1)S(1)} %convert_ele, ...), kind=kLoop, calls=%fused_computation.175 | loop fusion | bytes 4194336 | tf_op jit(solution)/shard_map/dynamic-slice.7
  140.2 4.5 %collective-permute-done.2 = bf16[32,8,512]{2,1,0:T(8,128)(2,1)S(1)} collective-permute-done((bf16[32,8,512]{2,1,0:T(8,128)(2,1)S(1)}, bf16[32,8,512]{2,1,0:T(8,128)(2,1)S(1)}, u32[]{:S(2)}, u32[]{:S(2)}) %collective-permute-start.2) | collective-permute-done | bytes 262176 | tf_op jit(solution)/shard_map/ppermute | solution.py:34
  144.7 4.8 %collective-permute-done.3 = bf16[32,8,512]{2,1,0:T(8,128)(2,1)S(1)} collective-permute-done((bf16[32,8,512]{2,1,0:T(8,128)(2,1)S(1)}, bf16[32,8,512]{2,1,0:T(8,128)(2,1)S(1)}, u32[]{:S(2)}, u32[]{:S(2)}) %collective-permute-start.3) | collective-permute-done | bytes 262176 | tf_op jit(solution)/shard_map/ppermute | solution.py:34
  149.6 12.9 %collective-permute-done.5 = bf16[32,8,512]{2,1,0:T(8,128)(2,1)S(1)} collective-permute-done((bf16[32,8,512]{2,1,0:T(8,128)(2,1)S(1)}, bf16[32,8,512]{2,1,0:T(8,128)(2,1)S(1)}, u32[]{:S(2)}, u32[]{:S(2)}) %collective-permute-start.5) | collective-permute-done | bytes 262176 | tf_op jit(solution)/shard_map/ppermute | solution.py:34
  164.6 19.7 %fusion.5 = bf16[4096,512]{0,1:T(8,128)(2,1)} fusion(bf16[2048,4096]{1,0:T(8,128)(2,1)} %param.15, f32[3,2048,512]{2,1,0:T(8,128)} %copy-done.2, bf16[2048,512]{1,0:T(8,128)(2,1)} %bitcast.176, f32[2048]{0:T(1024)S(1)} %copy-done.7, pred[512]{0:T(512)(128)(4,1)S(1)} %iota_compare_fusion), kind=kOutput, calls=%fused_computation.11 | convolution fusion | flops 8600420352 | bytes 35660288 | tf_op jit(solution)/shard_map/dot_general | solution.py:161
  184.3 76.4 %reduce-scatter.2.cloned.1.call-done = bf16[1024,512]{0,1:T(8,128)(2,1)} async-done(((bf16[4096,512]{0,1:T(8,128)(2,1)}), bf16[1024,512]{0,1:T(8,128)(2,1)}) %reduce-scatter.2.cloned.1.call-update) | async-done | bytes 1048592 | tf_op jit(solution)/shard_map/reduce_scatter | solution.py:160
  260.7 2.3 copy.48
  (83 shorter events, 13.8 us)
Async XLA Ops:
  6.5 42.8 %copy-start = (f32[16,256]{1,0:T(8,128)S(1)}, f32[16,256]{1,0:T(8,128)}, u32[]{:S(2)}) copy-start(f32[16,256]{1,0:T(8,128)} %param.13) | copy-start | bytes 49156
  7.2 5.8 %copy-start.5 = (f32[3,3,2048]{2,1,0:T(4,128)S(1)}, f32[3,3,2048]{2,1,0:T(4,128)}, u32[]{:S(2)}) copy-start(f32[3,3,2048]{2,1,0:T(4,128)} %param.9) | copy-start | bytes 221188
  7.2 6.5 %copy-start.8 = (u32[32]{0:T(128)S(1)}, u32[32]{0:T(128)}, u32[]{:S(2)}) copy-start(u32[32]{0:T(128)} %constant.53) | copy-start | bytes 388
  7.2 17.7 %copy-start.6 = (f32[16,256]{1,0:T(8,128)S(1)}, f32[16,256]{1,0:T(8,128)}, u32[]{:S(2)}) copy-start(f32[16,256]{1,0:T(8,128)} %param.12) | copy-start | bytes 49156
  10.6 14.5 %collective-permute-start = (bf16[3,2048,2]{1,0,2:T(4,128)(2,1)S(1)}, bf16[3,2048,2]{1,0,2:T(4,128)(2,1)S(1)}, u32[]{:S(2)}, u32[]{:S(2)}) collective-permute-start(bf16[3,2048,2]{1,0,2:T(4,128)(2,1)S(1)} %copy.53), channel_id=1, source_target_pairs={{0,4},{4,8},{8,12},{12,16},{16,20},{20,24},{24,28},{1,5},{5,9},{9,... | collective-permute-start | bytes 73736 | tf_op jit(solution)/shard_map/ppermute | solution.py:47
  38.7 4.5 %copy-start.2 = (f32[3,2048,512]{2,1,0:T(8,128)}, f32[3,2048,512]{2,1,0:T(8,128)S(1)}, u32[]{:S(2)}) copy-start(f32[3,2048,512]{2,1,0:T(8,128)S(1)} %multiply_add_fusion) | copy-start | bytes 37748740
  45.7 30.2 %all-to-all-start = ((bf16[256,8,512]{2,1,0:T(8,128)(2,1)}), bf16[256,8,512]{2,1,0:T(8,128)(2,1)S(1)}, u32[]{:S(2)}, u32[]{:S(2)}) async-start(bf16[256,8,512]{2,1,0:T(8,128)(2,1)} %fusion.10), calls=%async_computation | async-start | bytes 4194304 | tf_op jit(solution)/shard_map/all_to_all | solution.py:141
  49.3 211.4 %reduce-scatter.2.cloned.1.call-start = ((), (), s32[]{:S(2)}) async-start(), calls=%async_computation.2 | async-start | bytes 5242880 | tf_op jit(solution)/shard_map/reduce_scatter | solution.py:160
  75.9 1.3 copy-start.3
  109.5 7.5 %copy-start.4 = (bf16[32,8,32,128]{3,2,1,0:T(8,128)(2,1)S(1)}, bf16[32,8,32,128]{3,2,1,0:T(8,128)(2,1)}, u32[]{:S(2)}) copy-start(bf16[32,8,32,128]{3,2,1,0:T(8,128)(2,1)} %reshape.366) | copy-start | bytes 6291460
  135.4 4.1 %collective-permute-start.1 = (bf16[32,8,512]{2,1,0:T(8,128)(2,1)S(1)}, bf16[32,8,512]{2,1,0:T(8,128)(2,1)S(1)}, u32[]{:S(2)}, u32[]{:S(2)}) collective-permute-start(bf16[32,8,512]{2,1,0:T(8,128)(2,1)S(1)} %bitcast.183), channel_id=1, source_target_pairs={{0,4},{4,0},{8,12},{12,8},{16,20},{20,16},{24,28},{28,24},{1,5},{5... | collective-permute-start | bytes 786440 | tf_op jit(solution)/shard_map/ppermute | solution.py:34
  135.5 9.2 %collective-permute-start.2 = (bf16[32,8,512]{2,1,0:T(8,128)(2,1)S(1)}, bf16[32,8,512]{2,1,0:T(8,128)(2,1)S(1)}, u32[]{:S(2)}, u32[]{:S(2)}) collective-permute-start(bf16[32,8,512]{2,1,0:T(8,128)(2,1)S(1)} %bitcast.182), channel_id=1, source_target_pairs={{0,8},{4,12},{8,0},{12,4},{16,24},{20,28},{24,16},{28,20},{1,9},{5... | collective-permute-start | bytes 786440 | tf_op jit(solution)/shard_map/ppermute | solution.py:34
  136.2 13.3 %collective-permute-start.3 = (bf16[32,8,512]{2,1,0:T(8,128)(2,1)S(1)}, bf16[32,8,512]{2,1,0:T(8,128)(2,1)S(1)}, u32[]{:S(2)}, u32[]{:S(2)}) collective-permute-start(bf16[32,8,512]{2,1,0:T(8,128)(2,1)S(1)} %bitcast.181), channel_id=1, source_target_pairs={{0,12},{4,8},{8,4},{12,0},{16,28},{20,24},{24,20},{28,16},{1,13},{... | collective-permute-start | bytes 786440 | tf_op jit(solution)/shard_map/ppermute | solution.py:34
  137.6 11.9 %collective-permute-start.4 = (bf16[32,8,512]{2,1,0:T(8,128)(2,1)S(1)}, bf16[32,8,512]{2,1,0:T(8,128)(2,1)S(1)}, u32[]{:S(2)}, u32[]{:S(2)}) collective-permute-start(bf16[32,8,512]{2,1,0:T(8,128)(2,1)S(1)} %bitcast.180), channel_id=1, source_target_pairs={{0,16},{4,20},{8,24},{12,28},{16,0},{20,4},{24,8},{28,12},{1,17},{... | collective-permute-start | bytes 786440 | tf_op jit(solution)/shard_map/ppermute | solution.py:34
  138.3 24.2 %collective-permute-start.5 = (bf16[32,8,512]{2,1,0:T(8,128)(2,1)S(1)}, bf16[32,8,512]{2,1,0:T(8,128)(2,1)S(1)}, u32[]{:S(2)}, u32[]{:S(2)}) collective-permute-start(bf16[32,8,512]{2,1,0:T(8,128)(2,1)S(1)} %bitcast.179), channel_id=1, source_target_pairs={{0,20},{4,16},{8,28},{12,24},{16,4},{20,0},{24,12},{28,8},{1,21},{... | collective-permute-start | bytes 786440 | tf_op jit(solution)/shard_map/ppermute | solution.py:34
  139.6 22.9 %collective-permute-start.6 = (bf16[32,8,512]{2,1,0:T(8,128)(2,1)S(1)}, bf16[32,8,512]{2,1,0:T(8,128)(2,1)S(1)}, u32[]{:S(2)}, u32[]{:S(2)}) collective-permute-start(bf16[32,8,512]{2,1,0:T(8,128)(2,1)S(1)} %bitcast.178), channel_id=1, source_target_pairs={{0,24},{4,28},{8,16},{12,20},{16,8},{20,12},{24,0},{28,4},{1,25},{... | collective-permute-start | bytes 786440 | tf_op jit(solution)/shard_map/ppermute | solution.py:34
  144.7 17.8 %collective-permute-start.7 = (bf16[32,8,512]{2,1,0:T(8,128)(2,1)S(1)}, bf16[32,8,512]{2,1,0:T(8,128)(2,1)S(1)}, u32[]{:S(2)}, u32[]{:S(2)}) collective-permute-start(bf16[32,8,512]{2,1,0:T(8,128)(2,1)S(1)} %bitcast.177), channel_id=1, source_target_pairs={{0,28},{4,24},{8,20},{12,16},{16,12},{20,8},{24,4},{28,0},{1,29},{... | collective-permute-start | bytes 786440 | tf_op jit(solution)/shard_map/ppermute | solution.py:34
  162.6 2.0 copy-start.7
  184.3 78.7 %copy-start.1 = (f32[16,256]{1,0:T(8,128)S(1)}, f32[16,256]{1,0:T(8,128)}, u32[]{:S(2)}) copy-start(f32[16,256]{1,0:T(8,128)} %param.13) | copy-start | bytes 49156
Sparse Core Ops, SparseCore 0:
  184.4 76.2 reduce-scatter.1
